TPU v7x, 32 devices: a whole 2x2x4 slice. The times are simulated.
32 devices in a mesh: prow: 4 (over y, core), pcol: 8 (over z, x).
Axes of the slice: x: 2, y: 2, z: 4, core: 2. Of those that a mesh axis runs over, the one named last changes fastest.
Arguments:
- ainv: bfloat16 [8192, 8192], P('prow', 'pcol'), may hold values from -6 to 6
- panels: bfloat16 [3, 8192, 128], P(None, ('prow', 'pcol')), may hold values from -0.0625 to 0.0625
- structure: int32 [3, 64], replicated, may hold values from 0 to 1, as said below
- dinv: float32 [3, 128, 128], replicated, may hold values from -6 to 6
- couple: bfloat16 [2, 128, 128], replicated, may hold values from -0.5 to 0.5
Outputs:
- inv_panels: float32 [3, 8192, 128], P(None, ('prow', 'pcol'))
- inv_parent: float32 [2, 128, 128], replicated
- inv_diag: float32 [3, 128, 128], replicated
Inputs may be any that keep to these rules, and one draw needn't show every extreme that they name: Entries are 0 or 1; a block in the structure of step k+1 is also in that of step k.
All inputs are finite; a program needn't handle non-finite values.
Results may differ from a plain program's by a relative error of at most 0.0003.
Values may be sent and summed in bfloat16 or wider, within the bound.
No kernel may reach another device: no remote copies, remote signals or barrier semaphores. Data moves between devices by JAX's collectives and lax.ppermute only.
A program may use at most 64 MiB of HBM per device.

v0:
```python
import jax
import jax.numpy as jnp
from jax import lax
from jax.sharding import PartitionSpec as P


def broadcast(value, axis, source):
    kept = jnp.where(lax.axis_index(axis) == source, value, 0).astype(value.dtype)
    return lax.psum(kept, axis)


def shards(ainv, panels, structure, dinv, couple):
    high = lax.Precision.HIGHEST
    n_col = lax.axis_size("pcol")
    seg_rows = panels.shape[1]
    width_cols = panels.shape[2]
    sections = panels.shape[0]
    col_span = ainv.shape[1]
    height = ainv.shape[0]
    flat_index = lax.axis_index("prow") * n_col + lax.axis_index("pcol")
    row_ids = flat_index * seg_rows + jnp.arange(seg_rows, dtype=jnp.int32)
    block_ids = jnp.arange(structure.shape[1], dtype=jnp.int32)
    onehot = (row_ids[:, None] // width_cols == block_ids[None, :]).astype(jnp.float32)
    live_rows = jnp.einsum("rb,kb->kr", onehot, structure.astype(jnp.float32))
    factor = panels * live_rows[:, :, None].astype(jnp.bfloat16)
    column = lax.axis_index("pcol")
    offset = column * col_span % height
    owner = column * col_span // height
    products = []
    for section in range(sections):
        gathered = lax.all_gather(factor[section], "pcol", axis=0, tiled=True)
        wanted = lax.dynamic_slice_in_dim(gathered, offset, col_span, 0)
        received = broadcast(wanted, "prow", owner)

        def single_term(row_start, row_count, panel_cols=received):
            return jnp.dot(ainv, panel_cols, preferred_element_type=jnp.float32)

        products.append(
            lax.psum_scatter(
                single_term(jnp.int32(0), seg_rows * lax.axis_size("pcol")),
                "pcol",
                scatter_dimension=0,
                tiled=True,
            )
        )
    factor_wide = factor.astype(jnp.float32)
    couple_wide = couple.astype(jnp.float32)
    first_block = -products[0] * live_rows[0][:, None]
    first_local = jnp.dot(factor_wide[0].T, first_block, precision=high)
    diag_now = dinv[0] - lax.psum(first_local, ("prow", "pcol"))
    blocks_out = [first_block]
    diag_out = [diag_now]
    cross_out = []
    for section in range(1, sections):
        previous = blocks_out[-1]
        current = (
            -(products[section] + jnp.dot(previous, couple_wide[section - 1], precision=high))
            * live_rows[section][:, None]
        )
        own_term = jnp.dot(factor_wide[section].T, current, precision=high)
        cross_term = jnp.dot(previous.T, factor_wide[section], precision=high)
        own_sum, cross_sum = lax.psum((own_term, cross_term), ("prow", "pcol"))
        cross = -(cross_sum + jnp.dot(diag_now, couple_wide[section - 1], precision=high))
        diag_now = (
            dinv[section] - own_sum - jnp.dot(couple_wide[section - 1].T, cross, precision=high)
        )
        blocks_out.append(current)
        cross_out.append(cross)
        diag_out.append(diag_now)
    return (jnp.stack(blocks_out), jnp.stack(cross_out), jnp.stack(diag_out))


def solution(mesh):
    return jax.shard_map(
        shards,
        mesh=mesh,
        in_specs=(P("prow", "pcol"), P(None, ("prow", "pcol"), None), P(), P(), P()),
        out_specs=(P(None, ("prow", "pcol"), None), P(), P()),
        check_vma=False,
    )
```

profile of v0, /device:TPU:8, one launch (start us, length us, event | category | flops | bytes accessed | tf_op | source)
XLA Modules:
  0.0 495.4 jit_solution(17148334694424355662)
XLA Ops:
  7.3 0.9 fusion.45
  8.2 1.1 broadcast_multiply_fusion
  9.3 28.8 %all-gather = bf16[1,2048,128]{2,1,0:T(8,128)(2,1)S(1)} all-gather(bf16[1,256,128]{2,1,0:T(8,128)(2,1)S(1)} %get-tuple-element.14), channel_id=2, replica_groups=mesh['prow'=4,'pcol'=8] {'pcol'}, dimensions={1}, use_global_device_ids=true | all-gather | bytes 589824 | tf_op jit(solution)/shard_map/all_gather | solution.py:31
  38.0 31.6 %all-gather.2 = bf16[1,2048,128]{2,1,0:T(8,128)(2,1)S(1)} all-gather(bf16[1,256,128]{2,1,0:T(8,128)(2,1)S(1)} %get-tuple-element.15), channel_id=4, replica_groups=mesh['prow'=4,'pcol'=8] {'pcol'}, dimensions={1}, use_global_device_ids=true | all-gather | bytes 589824 | tf_op jit(solution)/shard_map/all_gather | solution.py:31
  71.2 31.1 %all-gather.1 = bf16[1,2048,128]{2,1,0:T(8,128)(2,1)S(1)} all-gather(bf16[1,256,128]{2,1,0:T(8,128)(2,1)S(1)} %get-tuple-element.16), channel_id=3, replica_groups=mesh['prow'=4,'pcol'=8] {'pcol'}, dimensions={1}, use_global_device_ids=true | all-gather | bytes 589824 | tf_op jit(solution)/shard_map/all_gather | solution.py:31
  103.1 39.1 %all-reduce.7.cloned.1.call-done = (bf16[1024,128]{1,0:T(8,128)(2,1)}, bf16[1024,128]{1,0:T(8,128)(2,1)}, bf16[1024,128]{1,0:T(8,128)(2,1)}) async-done(((bf16[1024,128]{1,0:T(8,128)(2,1)}, bf16[1024,128]{1,0:T(8,128)(2,1)}, bf16[1024,128]{1,0:T(8,128)(2,1)}), (bf16[1024,128]{1,0:T(8,128)(2,1)}, bf16[1024,128]{1,0:T(8,128)(2,1)}, bf16[1024,128]{1,0:T(8,128)(2,1)})) %all-reduce.7.cloned.1.call-update) | async-done | bytes 786448 | tf_op jit(solution)/shard_map/psum | solution.py:9
  142.2 4.8 convolution_bitcast_fusion.1
  147.1 4.7 convolution_bitcast_fusion.2
  151.9 4.8 convolution_bitcast_fusion
  156.7 54.9 %reduce-scatter.6.cloned.1.call-done = f32[256,128]{0,1:T(8,128)} async-done(((f32[2048,128]{0,1:T(8,128)}), f32[256,128]{0,1:T(8,128)}) %reduce-scatter.6.cloned.1.call-update) | async-done | bytes 131088 | tf_op jit(solution)/shard_map/reduce_scatter | solution.py:39
  211.7 67.1 %reduce-scatter.4.cloned.1.call-done = f32[256,128]{0,1:T(8,128)} async-done(((f32[2048,128]{0,1:T(8,128)}), f32[256,128]{0,1:T(8,128)}) %reduce-scatter.4.cloned.1.call-update) | async-done | bytes 131088 | tf_op jit(solution)/shard_map/reduce_scatter | solution.py:39
  278.8 1.2 fusion.2
  281.7 64.0 %reduce-scatter.8.cloned.1.call-done = f32[256,128]{0,1:T(8,128)} async-done(((f32[2048,128]{0,1:T(8,128)}), f32[256,128]{0,1:T(8,128)}) %reduce-scatter.8.cloned.1.call-update) | async-done | bytes 131088 | tf_op jit(solution)/shard_map/reduce_scatter | solution.py:39
  345.7 1.2 fusion.3
  346.9 0.9 fusion.14
  347.8 1.7 fusion.10
  349.5 1.8 fusion.9
  351.3 0.9 fusion.11
  352.3 0.9 copy.12
  353.2 129.2 %all-reduce.5.cloned.1.call-done = (f32[128,128]{1,0:T(8,128)}, f32[128,128]{1,0:T(8,128)}, f32[128,128]{1,0:T(8,128)}, f32[128,128]{1,0:T(8,128)}, f32[128,128]{1,0:T(8,128)}) async-done(((f32[128,128]{1,0:T(8,128)}, f32[128,128]{1,0:T(8,128)}, f32[128,128]{1,0:T(8,128)}, f32[128,128]{1,0:T(8,128)}, f32[128,128]{1,0:T(8,128)}), (f32[128,128]{1,0:T(8,128)}, f32[128,128]{1,0:T(8,128)}, f32[128,128]{1,0:T(8,128)}, ...) | async-done | bytes 327696 | tf_op jit(solution)/shard_map/psum | solution.py:62
  483.2 1.0 fusion.8
  484.3 1.1 fusion.7
  485.4 1.0 fusion.6
  486.4 1.1 fusion.5
  (30 shorter events, 6.5 us)
Async XLA Ops:
  7.2 135.0 %all-reduce.7.cloned.1.call-start = ((), (), s32[]{:S(2)}) async-start(), calls=%async_computation.7 | async-start | bytes 1572864 | tf_op jit(solution)/shard_map/psum | solution.py:9
  103.1 108.6 %reduce-scatter.6.cloned.1.call-start = ((), (), s32[]{:S(2)}) async-start(), calls=%async_computation.4 | async-start | bytes 1179648 | tf_op jit(solution)/shard_map/reduce_scatter | solution.py:39
  142.2 4.9 copy-start.3
  147.0 4.9 copy-start.2
  147.0 131.7 %reduce-scatter.4.cloned.1.call-start = ((), (), s32[]{:S(2)}) async-start(), calls=%async_computation.3 | async-start | bytes 1179648 | tf_op jit(solution)/shard_map/reduce_scatter | solution.py:39
  151.8 127.0 %copy-start = (bf16[2,128,128]{2,1,0:T(8,128)(2,1)S(1)}, bf16[2,128,128]{2,1,0:T(8,128)(2,1)}, u32[]{:S(2)}) copy-start(bf16[2,128,128]{2,1,0:T(8,128)(2,1)} %param.9) | copy-start | bytes 196612
  151.8 193.9 %reduce-scatter.8.cloned.1.call-start = ((), (), s32[]{:S(2)}) async-start(), calls=%async_computation.5 | async-start | bytes 1179648 | tf_op jit(solution)/shard_map/reduce_scatter | solution.py:39
  151.9 330.5 %copy-start.1 = (f32[3,128,128]{2,1,0:T(8,128)S(1)}, f32[3,128,128]{2,1,0:T(8,128)}, u32[]{:S(2)}) copy-start(f32[3,128,128]{2,1,0:T(8,128)} %param.8) | copy-start | bytes 589828
  156.7 325.7 %all-reduce.5.cloned.1.call-start = ((), (), s32[]{:S(2)}) async-start(), calls=%async_computation.6 | async-start | bytes 655360 | tf_op jit(solution)/shard_map/psum | solution.py:62
Sparse Core Ops, SparseCore 0:
  103.2 38.9 all-reduce.6
  147.2 64.4 reduce-scatter.5
  215.1 63.6 reduce-scatter.3
  282.0 63.6 reduce-scatter.7
  352.4 129.9 all-reduce.4
where the time goes:
time: 496 us; the launch traced here: 495 us
  waiting for transfers between devices  354 us (71%)
  blocking collectives  91.5 us (18%)
  matrix products  27.9 us (6%)
  between operations  13.9 us (3%)
  other arithmetic  6.52 us (1%)
    reduce_scatter x3, waiting for transfers between devices, shards(): lax.psum_scatter(single_term(jnp.int32(0), seg_rows * lax.axis_size('pcol...  186 us
    psum x1, waiting for transfers between devices, shards(): own_sum, cross_sum = lax.psum((own_term, cross_term), ('prow', 'pcol'))  129 us
    all_gather x3, blocking collectives, shards(): gathered = lax.all_gather(factor[section], 'pcol', axis=0, tiled=True)  91.5 us
    psum x1, waiting for transfers between devices, broadcast(): return lax.psum(kept, axis)  39.1 us
    dot_general x3, matrix products, single_term(): return jnp.dot(ainv, panel_cols, preferred_element_type=jnp.float32)  14.3 us
  transfers between devices with their start and end apart: 5, of which 5 were waited for; matrix products, arithmetic and copies ran while one was open for 3% of the time, Pallas kernels for 0%

commit v1 on v0

--- a/solution.py
+++ b/solution.py
@@ -2,6 +2,28 @@
 import jax.numpy as jnp
 from jax import lax
 from jax.sharding import PartitionSpec as P
+
+
+def joined_along(parts, dim):
+    parts = jnp.moveaxis(parts, 0, dim)
+    shape = parts.shape
+    return parts.reshape(*shape[:dim], shape[dim] * shape[dim + 1], *shape[dim + 2 :])
+
+
+def gather_around(array, axis, dim):
+    size = lax.axis_size(axis)
+    pairs = [(i, (i + 1) % size) for i in range(size)]
+    back = [(b, a) for a, b in pairs]
+    lower, upper = ([], [])
+    for step in range(size - 1):
+        if step % 2 == 0:
+            lower.append(lax.ppermute(lower[-1] if lower else array, axis, pairs))
+        else:
+            upper.append(lax.ppermute(upper[-1] if upper else array, axis, back))
+    pieces = jnp.stack([*lower[::-1], array, *upper])
+    shift = lax.axis_index(axis) - len(lower)
+    pieces = pieces[(jnp.arange(size) - shift) % size]
+    return joined_along(pieces, dim)
 
 
 def broadcast(value, axis, source):
@@ -28,7 +50,7 @@
     owner = column * col_span // height
     products = []
     for section in range(sections):
-        gathered = lax.all_gather(factor[section], "pcol", axis=0, tiled=True)
+        gathered = gather_around(factor[section], "pcol", 0)
         wanted = lax.dynamic_slice_in_dim(gathered, offset, col_span, 0)
         received = broadcast(wanted, "prow", owner)
 

time: 496 us -> 440 us (0.89)
  blocking collectives: 91.5 us -> 0 us
  starting transfers between devices: 0.21 us -> 29.5 us
  waiting for transfers between devices: 354 us -> 359 us
    all_gather x3 -> x0, blocking collectives: 91.5 us -> none  [shards(): gathered = lax.all_gather(factor[section], 'pcol', axis=0, tiled=True)]
    ppermute x0 -> x21, starting transfers between devices: none -> 29.3 us  [the longest x9 15.8 us: gather_around(): upper.append(lax.ppermute(upper[-1] if upper else array, axis, back))]
    ppermute x0 -> x21, waiting for transfers between devices: none -> 8.57 us  [the longest x12 5.69 us: gather_around(): lower.append(lax.ppermute(lower[-1] if lower else array, axis, pairs))]
  transfers between devices with their start and end apart: 5 -> 26, of which waited for: 5 -> 9; matrix products, arithmetic and copies ran while one was open for 3% -> 4% of each run, Pallas kernels for 0% -> 0%
where the time goes in v1:
time: 440 us
  waiting for transfers between devices  359 us (82%)
  starting transfers between devices  29.5 us (7%)
  matrix products  27.9 us (6%)
  between operations  14.1 us (3%)
  other arithmetic  5.92 us (1%)
    reduce_scatter x3, waiting for transfers between devices, shards(): lax.psum_scatter(single_term(jnp.int32(0), seg_rows * lax.axis_size('pcol...  186 us
    psum x1, waiting for transfers between devices, shards(): own_sum, cross_sum = lax.psum((own_term, cross_term), ('prow', 'pcol'))  129 us
    psum x1, waiting for transfers between devices, broadcast(): return lax.psum(kept, axis)  35.1 us
    ppermute x9, starting transfers between devices, gather_around(): upper.append(lax.ppermute(upper[-1] if upper else array, axis, back))  15.8 us
    dot_general x3, matrix products, single_term(): return jnp.dot(ainv, panel_cols, preferred_element_type=jnp.float32)  14.3 us
    ppermute x12, starting transfers between devices, gather_around(): lower.append(lax.ppermute(lower[-1] if lower else array, axis, pairs))  13.5 us
  transfers between devices with their start and end apart: 26, of which 9 were waited for; matrix products, arithmetic and copies ran while one was open for 4% of the time, Pallas kernels for 0%

profile of v1, /device:TPU:8, one launch (start us, length us, event | category | flops | bytes accessed | tf_op | source)
XLA Modules:
  0.0 439.6 jit_solution(11782098868727066701)
XLA Ops:
  9.3 1.5 collective-permute-start.7
  10.8 1.5 collective-permute-start.14
  12.4 1.5 collective-permute-start
  15.8 1.5 collective-permute-start.8
  17.3 1.7 collective-permute-start.4
  19.6 2.1 collective-permute-start.1
  22.6 1.9 collective-permute-start.9
  24.5 2.2 collective-permute-done.4
  26.7 2.4 collective-permute-start.5
  29.1 2.5 collective-permute-start.2
  31.8 2.8 collective-permute-start.13
  34.6 4.2 collective-permute-start.20
  38.8 2.6 collective-permute-start.6
  41.5 5.0 %collective-permute-done.17 = bf16[256,128]{1,0:T(8,128)(2,1)S(1)} collective-permute-done((bf16[256,128]{1,0:T(8,128)(2,1)S(1)}, bf16[256,128]{1,0:T(8,128)(2,1)S(1)}, u32[]{:S(2)}, u32[]{:S(2)}) %collective-permute-start.17) | collective-permute-done | bytes 65568 | tf_op jit(solution)/shard_map/ppermute | solution.py:20
  51.2 35.1 %all-reduce.7.cloned.1.call-done = (bf16[1024,128]{1,0:T(8,128)(2,1)}, bf16[1024,128]{1,0:T(8,128)(2,1)}, bf16[1024,128]{1,0:T(8,128)(2,1)}) async-done(((bf16[1024,128]{1,0:T(8,128)(2,1)}, bf16[1024,128]{1,0:T(8,128)(2,1)}, bf16[1024,128]{1,0:T(8,128)(2,1)}), (bf16[1024,128]{1,0:T(8,128)(2,1)}, bf16[1024,128]{1,0:T(8,128)(2,1)}, bf16[1024,128]{1,0:T(8,128)(2,1)})) %all-reduce.7.cloned.1.call-update) | async-done | bytes 786448 | tf_op jit(solution)/shard_map/psum | solution.py:31
  86.4 4.8 %convolution_bitcast_fusion.2 = f32[2048,128]{0,1:T(8,128)} fusion(bf16[1024,128]{1,0:T(8,128)(2,1)} %get-tuple-element.13, bf16[2048,1024]{1,0:T(8,128)(2,1)} %param.5), kind=kOutput, calls=%fused_computation.5 | convolution fusion | flops 536870912 | bytes 5505024 | tf_op jit(solution)/shard_map/dot_general | solution.py:58
  91.3 4.7 %convolution_bitcast_fusion.1 = f32[2048,128]{0,1:T(8,128)} fusion(bf16[1024,128]{1,0:T(8,128)(2,1)S(1)} %copy-done.3, bf16[2048,1024]{1,0:T(8,128)(2,1)} %param.5), kind=kOutput, calls=%fused_computation.4 | convolution fusion | flops 536870912 | bytes 5505024 | tf_op jit(solution)/shard_map/dot_general | solution.py:58
  96.1 4.7 %convolution_bitcast_fusion = f32[2048,128]{0,1:T(8,128)} fusion(bf16[1024,128]{1,0:T(8,128)(2,1)S(1)} %copy-done.2, bf16[2048,1024]{1,0:T(8,128)(2,1)} %param.5), kind=kOutput, calls=%fused_computation.3 | convolution fusion | flops 536870912 | bytes 5505024 | tf_op jit(solution)/shard_map/dot_general | solution.py:58
  100.9 55.0 %reduce-scatter.4.cloned.1.call-done = f32[256,128]{0,1:T(8,128)} async-done(((f32[2048,128]{0,1:T(8,128)}), f32[256,128]{0,1:T(8,128)}) %reduce-scatter.4.cloned.1.call-update) | async-done | bytes 131088 | tf_op jit(solution)/shard_map/reduce_scatter | solution.py:61
  155.9 67.1 %reduce-scatter.6.cloned.1.call-done = f32[256,128]{0,1:T(8,128)} async-done(((f32[2048,128]{0,1:T(8,128)}), f32[256,128]{0,1:T(8,128)}) %reduce-scatter.6.cloned.1.call-update) | async-done | bytes 131088 | tf_op jit(solution)/shard_map/reduce_scatter | solution.py:61
  226.0 64.0 %reduce-scatter.8.cloned.1.call-done = f32[256,128]{0,1:T(8,128)} async-done(((f32[2048,128]{0,1:T(8,128)}), f32[256,128]{0,1:T(8,128)}) %reduce-scatter.8.cloned.1.call-update) | async-done | bytes 131088 | tf_op jit(solution)/shard_map/reduce_scatter | solution.py:61
  292.1 1.7 fusion.10
  293.8 1.8 fusion.9
  297.5 129.1 %all-reduce.5.cloned.1.call-done = (f32[128,128]{1,0:T(8,128)}, f32[128,128]{1,0:T(8,128)}, f32[128,128]{1,0:T(8,128)}, f32[128,128]{1,0:T(8,128)}, f32[128,128]{1,0:T(8,128)}) async-done(((f32[128,128]{1,0:T(8,128)}, f32[128,128]{1,0:T(8,128)}, f32[128,128]{1,0:T(8,128)}, f32[128,128]{1,0:T(8,128)}, f32[128,128]{1,0:T(8,128)}), (f32[128,128]{1,0:T(8,128)}, f32[128,128]{1,0:T(8,128)}, f32[128,128]{1,0:T(8,128)}, ...) | async-done | bytes 327696 | tf_op jit(solution)/shard_map/psum | solution.py:84
  (95 shorter events, 23.8 us)
Async XLA Ops:
  7.2 79.2 %all-reduce.7.cloned.1.call-start = ((), (), s32[]{:S(2)}) async-start(), calls=%async_computation.7 | async-start | bytes 1572864 | tf_op jit(solution)/shard_map/psum | solution.py:31
  9.3 6.5 %collective-permute-start.7 = (bf16[256,128]{1,0:T(8,128)(2,1)S(1)}, bf16[256,128]{1,0:T(8,128)(2,1)S(1)}, u32[]{:S(2)}, u32[]{:S(2)}) collective-permute-start(bf16[256,128]{1,0:T(8,128)(2,1)S(1)} %get-tuple-element.19), channel_id=1, source_target_pairs={{0,1},{1,2},{2,3},{3,4},{4,5},{5,6},{6,7},{7,0},{8,9},{9,10},{10,1... | collective-permute-start | bytes 196616 | tf_op jit(solution)/shard_map/ppermute | solution.py:20
  10.8 6.5 %collective-permute-start.14 = (bf16[256,128]{1,0:T(8,128)(2,1)S(1)}, bf16[256,128]{1,0:T(8,128)(2,1)S(1)}, u32[]{:S(2)}, u32[]{:S(2)}) collective-permute-start(bf16[256,128]{1,0:T(8,128)(2,1)S(1)} %get-tuple-element.18), channel_id=1, source_target_pairs={{0,1},{1,2},{2,3},{3,4},{4,5},{5,6},{6,7},{7,0},{8,9},{9,10},{10,1... | collective-permute-start | bytes 196616 | tf_op jit(solution)/shard_map/ppermute | solution.py:20
  12.4 6.7 %collective-permute-start = (bf16[256,128]{1,0:T(8,128)(2,1)S(1)}, bf16[256,128]{1,0:T(8,128)(2,1)S(1)}, u32[]{:S(2)}, u32[]{:S(2)}) collective-permute-start(bf16[256,128]{1,0:T(8,128)(2,1)S(1)} %get-tuple-element.17), channel_id=1, source_target_pairs={{0,1},{1,2},{2,3},{3,4},{4,5},{5,6},{6,7},{7,0},{8,9},{9,10},{10,1... | collective-permute-start | bytes 196616 | tf_op jit(solution)/shard_map/ppermute | solution.py:20
  13.8 5.8 %collective-permute-start.11 = (bf16[256,128]{1,0:T(8,128)(2,1)S(1)}, bf16[256,128]{1,0:T(8,128)(2,1)S(1)}, u32[]{:S(2)}, u32[]{:S(2)}) collective-permute-start(bf16[256,128]{1,0:T(8,128)(2,1)S(1)} %get-tuple-element.19), channel_id=1, source_target_pairs={{1,0},{2,1},{3,2},{4,3},{5,4},{6,5},{7,6},{0,7},{9,8},{10,9},{11,1... | collective-permute-start | bytes 196616 | tf_op jit(solution)/shard_map/ppermute | solution.py:22
  15.3 7.2 %collective-permute-start.18 = (bf16[256,128]{1,0:T(8,128)(2,1)S(1)}, bf16[256,128]{1,0:T(8,128)(2,1)S(1)}, u32[]{:S(2)}, u32[]{:S(2)}) collective-permute-start(bf16[256,128]{1,0:T(8,128)(2,1)S(1)} %get-tuple-element.18), channel_id=1, source_target_pairs={{1,0},{2,1},{3,2},{4,3},{5,4},{6,5},{7,6},{0,7},{9,8},{10,9},{11,1... | collective-permute-start | bytes 196616 | tf_op jit(solution)/shard_map/ppermute | solution.py:22
  15.8 6.8 %collective-permute-start.8 = (bf16[256,128]{1,0:T(8,128)(2,1)S(1)}, bf16[256,128]{1,0:T(8,128)(2,1)S(1)}, u32[]{:S(2)}, u32[]{:S(2)}) collective-permute-start(bf16[256,128]{1,0:T(8,128)(2,1)S(1)} %collective-permute-done.7), channel_id=1, source_target_pairs={{0,1},{1,2},{2,3},{3,4},{4,5},{5,6},{6,7},{7,0},{8,9},{9,10},{10,1... | collective-permute-start | bytes 196616 | tf_op jit(solution)/shard_map/ppermute | solution.py:20
  17.3 9.3 %collective-permute-start.4 = (bf16[256,128]{1,0:T(8,128)(2,1)S(1)}, bf16[256,128]{1,0:T(8,128)(2,1)S(1)}, u32[]{:S(2)}, u32[]{:S(2)}) collective-permute-start(bf16[256,128]{1,0:T(8,128)(2,1)S(1)} %get-tuple-element.17), channel_id=1, source_target_pairs={{1,0},{2,1},{3,2},{4,3},{5,4},{6,5},{7,6},{0,7},{9,8},{10,9},{11,1... | collective-permute-start | bytes 196616 | tf_op jit(solution)/shard_map/ppermute | solution.py:22
  19.1 7.6 %collective-permute-start.15 = (bf16[256,128]{1,0:T(8,128)(2,1)S(1)}, bf16[256,128]{1,0:T(8,128)(2,1)S(1)}, u32[]{:S(2)}, u32[]{:S(2)}) collective-permute-start(bf16[256,128]{1,0:T(8,128)(2,1)S(1)} %collective-permute-done.14), channel_id=1, source_target_pairs={{0,1},{1,2},{2,3},{3,4},{4,5},{5,6},{6,7},{7,0},{8,9},{9,10},{10,1... | collective-permute-start | bytes 196616 | tf_op jit(solution)/shard_map/ppermute | solution.py:20
  19.6 9.4 %collective-permute-start.1 = (bf16[256,128]{1,0:T(8,128)(2,1)S(1)}, bf16[256,128]{1,0:T(8,128)(2,1)S(1)}, u32[]{:S(2)}, u32[]{:S(2)}) collective-permute-start(bf16[256,128]{1,0:T(8,128)(2,1)S(1)} %collective-permute-done), channel_id=1, source_target_pairs={{0,1},{1,2},{2,3},{3,4},{4,5},{5,6},{6,7},{7,0},{8,9},{9,10},{10,1... | collective-permute-start | bytes 196616 | tf_op jit(solution)/shard_map/ppermute | solution.py:20
  22.4 6.7 %collective-permute-start.12 = (bf16[256,128]{1,0:T(8,128)(2,1)S(1)}, bf16[256,128]{1,0:T(8,128)(2,1)S(1)}, u32[]{:S(2)}, u32[]{:S(2)}) collective-permute-start(bf16[256,128]{1,0:T(8,128)(2,1)S(1)} %collective-permute-done.11), channel_id=1, source_target_pairs={{1,0},{2,1},{3,2},{4,3},{5,4},{6,5},{7,6},{0,7},{9,8},{10,9},{11,1... | collective-permute-start | bytes 196616 | tf_op jit(solution)/shard_map/ppermute | solution.py:22
  22.6 9.0 %collective-permute-start.9 = (bf16[256,128]{1,0:T(8,128)(2,1)S(1)}, bf16[256,128]{1,0:T(8,128)(2,1)S(1)}, u32[]{:S(2)}, u32[]{:S(2)}) collective-permute-start(bf16[256,128]{1,0:T(8,128)(2,1)S(1)} %collective-permute-done.8), channel_id=1, source_target_pairs={{0,1},{1,2},{2,3},{3,4},{4,5},{5,6},{6,7},{7,0},{8,9},{9,10},{10,1... | collective-permute-start | bytes 196616 | tf_op jit(solution)/shard_map/ppermute | solution.py:20
  26.7 8.0 %collective-permute-start.5 = (bf16[256,128]{1,0:T(8,128)(2,1)S(1)}, bf16[256,128]{1,0:T(8,128)(2,1)S(1)}, u32[]{:S(2)}, u32[]{:S(2)}) collective-permute-start(bf16[256,128]{1,0:T(8,128)(2,1)S(1)} %collective-permute-done.4), channel_id=1, source_target_pairs={{1,0},{2,1},{3,2},{4,3},{5,4},{6,5},{7,6},{0,7},{9,8},{10,9},{11,1... | collective-permute-start | bytes 196616 | tf_op jit(solution)/shard_map/ppermute | solution.py:22
  29.1 9.7 %collective-permute-start.16 = (bf16[256,128]{1,0:T(8,128)(2,1)S(1)}, bf16[256,128]{1,0:T(8,128)(2,1)S(1)}, u32[]{:S(2)}, u32[]{:S(2)}) collective-permute-start(bf16[256,128]{1,0:T(8,128)(2,1)S(1)} %collective-permute-done.15), channel_id=1, source_target_pairs={{0,1},{1,2},{2,3},{3,4},{4,5},{5,6},{6,7},{7,0},{8,9},{9,10},{10,1... | collective-permute-start | bytes 196616 | tf_op jit(solution)/shard_map/ppermute | solution.py:20
  29.1 12.3 %collective-permute-start.2 = (bf16[256,128]{1,0:T(8,128)(2,1)S(1)}, bf16[256,128]{1,0:T(8,128)(2,1)S(1)}, u32[]{:S(2)}, u32[]{:S(2)}) collective-permute-start(bf16[256,128]{1,0:T(8,128)(2,1)S(1)} %collective-permute-done.1), channel_id=1, source_target_pairs={{0,1},{1,2},{2,3},{3,4},{4,5},{5,6},{6,7},{7,0},{8,9},{9,10},{10,1... | collective-permute-start | bytes 196616 | tf_op jit(solution)/shard_map/ppermute | solution.py:20
  31.6 9.8 %collective-permute-start.10 = (bf16[256,128]{1,0:T(8,128)(2,1)S(1)}, bf16[256,128]{1,0:T(8,128)(2,1)S(1)}, u32[]{:S(2)}, u32[]{:S(2)}) collective-permute-start(bf16[256,128]{1,0:T(8,128)(2,1)S(1)} %collective-permute-done.9), channel_id=1, source_target_pairs={{0,1},{1,2},{2,3},{3,4},{4,5},{5,6},{6,7},{7,0},{8,9},{9,10},{10,1... | collective-permute-start | bytes 196616 | tf_op jit(solution)/shard_map/ppermute | solution.py:20
  31.8 15.7 %collective-permute-start.13 = (bf16[256,128]{1,0:T(8,128)(2,1)S(1)}, bf16[256,128]{1,0:T(8,128)(2,1)S(1)}, u32[]{:S(2)}, u32[]{:S(2)}) collective-permute-start(bf16[256,128]{1,0:T(8,128)(2,1)S(1)} %collective-permute-done.12), channel_id=1, source_target_pairs={{1,0},{2,1},{3,2},{4,3},{5,4},{6,5},{7,6},{0,7},{9,8},{10,9},{11,1... | collective-permute-start | bytes 196616 | tf_op jit(solution)/shard_map/ppermute | solution.py:22
  34.6 12.9 %collective-permute-start.20 = (bf16[256,128]{1,0:T(8,128)(2,1)S(1)}, bf16[256,128]{1,0:T(8,128)(2,1)S(1)}, u32[]{:S(2)}, u32[]{:S(2)}) collective-permute-start(bf16[256,128]{1,0:T(8,128)(2,1)S(1)} %collective-permute-done.19), channel_id=1, source_target_pairs={{1,0},{2,1},{3,2},{4,3},{5,4},{6,5},{7,6},{0,7},{9,8},{10,9},{11,1... | collective-permute-start | bytes 196616 | tf_op jit(solution)/shard_map/ppermute | solution.py:22
  38.8 10.1 %collective-permute-start.6 = (bf16[256,128]{1,0:T(8,128)(2,1)S(1)}, bf16[256,128]{1,0:T(8,128)(2,1)S(1)}, u32[]{:S(2)}, u32[]{:S(2)}) collective-permute-start(bf16[256,128]{1,0:T(8,128)(2,1)S(1)} %collective-permute-done.5), channel_id=1, source_target_pairs={{1,0},{2,1},{3,2},{4,3},{5,4},{6,5},{7,6},{0,7},{9,8},{10,9},{11,1... | collective-permute-start | bytes 196616 | tf_op jit(solution)/shard_map/ppermute | solution.py:22
  41.4 5.9 %collective-permute-start.3 = (bf16[256,128]{1,0:T(8,128)(2,1)S(1)}, bf16[256,128]{1,0:T(8,128)(2,1)S(1)}, u32[]{:S(2)}, u32[]{:S(2)}) collective-permute-start(bf16[256,128]{1,0:T(8,128)(2,1)S(1)} %collective-permute-done.2), channel_id=1, source_target_pairs={{0,1},{1,2},{2,3},{3,4},{4,5},{5,6},{6,7},{7,0},{8,9},{9,10},{10,1... | collective-permute-start | bytes 196616 | tf_op jit(solution)/shard_map/ppermute | solution.py:20
  51.2 104.8 %reduce-scatter.4.cloned.1.call-start = ((), (), s32[]{:S(2)}) async-start(), calls=%async_computation.3 | async-start | bytes 1179648 | tf_op jit(solution)/shard_map/reduce_scatter | solution.py:61
  91.2 131.8 %reduce-scatter.6.cloned.1.call-start = ((), (), s32[]{:S(2)}) async-start(), calls=%async_computation.4 | async-start | bytes 1179648 | tf_op jit(solution)/shard_map/reduce_scatter | solution.py:61
  96.0 194.0 %reduce-scatter.8.cloned.1.call-start = ((), (), s32[]{:S(2)}) async-start(), calls=%async_computation.5 | async-start | bytes 1179648 | tf_op jit(solution)/shard_map/reduce_scatter | solution.py:61
  100.9 325.7 %all-reduce.5.cloned.1.call-start = ((), (), s32[]{:S(2)}) async-start(), calls=%async_computation.6 | async-start | bytes 655360 | tf_op jit(solution)/shard_map/psum | solution.py:84
  (6 other events, 477.6 us)
Sparse Core Ops, SparseCore 0:
  51.3 35.0 all-reduce.6
  91.4 64.5 reduce-scatter.3
  159.4 63.6 reduce-scatter.5
  226.3 63.6 reduce-scatter.7
  296.6 129.9 all-reduce.4
